TPU v7x, 256 devices: a whole 4x4x8 slice. The times are simulated.
256 devices in a mesh: expert: 32 (over z, y), tensor: 4 (over x), dp: 2 (over core).
Axes of the slice: x: 4, y: 4, z: 8, core: 2. Of those that a mesh axis runs over, the one named last changes fastest.
Arguments:
- tokens: bfloat16 [1024, 7168], P(('expert', 'dp')), may hold values from -6 to 6
- expert_ids: int32 [1024, 8], P(('expert', 'dp')), may hold values from 0 to 31, all different within a row; in each aligned block of 16 rows (0 to 15, 16 to 31, ...) at most 8 rows name the same one
- route_scores: float32 [1024, 8], P(('expert', 'dp')), may hold values from 0.05 to 1
- gate_weight: bfloat16 [32, 7168, 2048], P('expert', 'dp', 'tensor'), may hold values from -0.0625 to 0.0625
- up_weight: bfloat16 [32, 7168, 2048], P('expert', 'dp', 'tensor'), may hold values from -0.0625 to 0.0625
- down_weight: bfloat16 [32, 2048, 7168], P('expert', 'tensor', 'dp'), may hold values from -0.125 to 0.125
Outputs:
- mixed: bfloat16 [1024, 2, 3584], P(('expert', 'dp'), None, 'tensor')
Inputs may be any that keep to these rules, and one draw needn't show every extreme that they name: `expert_ids`: each token names 8 different experts. In each aligned block of 16 tokens (the tokens of one device along expert and dp) no expert is named by more than 8 tokens, a bound that some block reaches.
All inputs are finite; a program needn't handle non-finite values.
Results may differ from a plain program's by a relative error of at most 0.02.
Values may be sent and summed in bfloat16 or wider, within the bound.
A program may use at most 64 MiB of HBM per device.

v0:
```python
import jax
import jax.numpy as jnp
from jax import lax
from jax.sharding import PartitionSpec as P

TOP = 8
EXPERTS = 32
CAP = 8


def route_over_experts(blocks):
    return lax.all_to_all(blocks, "expert", split_axis=2, concat_axis=2, tiled=True)


def block_tables(block_ids, expert_count):
    pair_ids = block_ids.reshape(-1)
    expert_hot = (pair_ids[:, None] == jnp.arange(EXPERTS, dtype=jnp.int32)[None, :]).astype(
        jnp.int32
    )
    earlier = jnp.cumsum(expert_hot, axis=0) - expert_hot
    slot_index = jnp.sum(earlier * expert_hot, axis=1).reshape(block_ids.shape)
    expert_onehot = (
        block_ids[:, :, None] == jnp.arange(EXPERTS, dtype=jnp.int32)[None, None, :]
    ).astype(jnp.float32)
    expert_onehot = expert_onehot.reshape(
        block_ids.shape[0], TOP, expert_count, EXPERTS // expert_count
    )
    slot_onehot = (
        slot_index[:, :, None] == jnp.arange(CAP, dtype=jnp.int32)[None, None, :]
    ).astype(jnp.float32)
    return (expert_onehot, slot_onehot)


def placing_table(block_ids, expert_count):
    expert_onehot, slot_onehot = block_tables(block_ids, expert_count)
    return jnp.einsum("tkgl,tkc->lgct", expert_onehot, slot_onehot).astype(jnp.bfloat16)


def mixing_table(block_ids, block_scores, expert_count):
    expert_onehot, slot_onehot = block_tables(block_ids, expert_count)
    weights = (2.5 * block_scores / jnp.sum(block_scores, axis=1, keepdims=True)).astype(
        jnp.bfloat16
    )
    return jnp.einsum(
        "tk,tkgl,tkc->tglc", weights.astype(jnp.float32), expert_onehot, slot_onehot
    ).astype(jnp.bfloat16)


def on_device(tokens, expert_ids, route_scores, gate_weight, up_weight, down_weight):
    expert_count = lax.axis_size("expert")
    dp_count = lax.axis_size("dp")
    local_experts = gate_weight.shape[0]
    block_tokens = expert_ids.shape[0]
    placing = placing_table(expert_ids, expert_count)
    split_rows = tokens.reshape(block_tokens, dp_count, tokens.shape[1] // dp_count)
    outgoing = jnp.einsum(
        "lgct,tpd->lpgcd", placing, split_rows, preferred_element_type=jnp.float32
    ).astype(jnp.bfloat16)
    halves = lax.all_to_all(outgoing, "dp", split_axis=1, concat_axis=1, tiled=True)
    half_width = halves.shape[4]
    arrived = route_over_experts(halves)
    arrived = arrived.reshape(local_experts, dp_count * expert_count * CAP, half_width)
    gate = jnp.einsum("lrh,lhf->lrf", arrived, gate_weight, preferred_element_type=jnp.float32)
    up = jnp.einsum("lrh,lhf->lrf", arrived, up_weight, preferred_element_type=jnp.float32)
    gate, up = (
        lax.psum(gate.astype(jnp.bfloat16), "dp").astype(jnp.float32),
        lax.psum(up.astype(jnp.bfloat16), "dp").astype(jnp.float32),
    )
    hidden = (jax.nn.silu(gate) * up).astype(jnp.bfloat16)
    partial_value = jnp.einsum(
        "lrf,lfh->lrh", hidden, down_weight, preferred_element_type=jnp.float32
    )
    summed = lax.psum_scatter(
        partial_value.astype(jnp.bfloat16), "tensor", scatter_dimension=2, tiled=True
    ).astype(jnp.float32)
    summed = summed.astype(jnp.bfloat16).reshape(
        local_experts, dp_count, expert_count, CAP, summed.shape[2]
    )
    returned = route_over_experts(summed)
    results = lax.all_to_all(returned, "dp", split_axis=1, concat_axis=1, tiled=True)
    mixing = mixing_table(expert_ids, route_scores, expert_count)
    mixed = jnp.einsum("tglc,lhgcd->thd", mixing, results, preferred_element_type=jnp.float32)
    return mixed.astype(jnp.bfloat16)


def solution(mesh):
    in_specs = (
        P(("expert", "dp"), None),
        P(("expert", "dp"), None),
        P(("expert", "dp"), None),
        P("expert", "dp", "tensor"),
        P("expert", "dp", "tensor"),
        P("expert", "tensor", "dp"),
    )
    out_specs = P(("expert", "dp"), None, "tensor")
    return jax.shard_map(
        on_device, mesh=mesh, in_specs=in_specs, out_specs=out_specs, check_vma=False
    )
```

profile of v0, /device:TPU:1, one launch (start us, length us, event | category | flops | bytes accessed | tf_op | source)
XLA Modules:
  0.0 278.3 jit_solution(17216406574727778507)
XLA Ops:
  6.5 0.0 all-reduce.3.cloned.1.call-start
  6.5 0.8 copy.22
  7.3 0.1 eq.28
  7.4 0.1 fusion.31
  7.5 0.2 reduce_window_sum.12
  7.7 0.2 select_reduce_fusion
  7.8 0.1 eq.32
  7.9 0.2 fusion.20
  8.1 0.1 copy.34
  8.3 2.0 fusion
  10.3 0.3 copy.27
  10.6 9.6 %all_to_all.20 = bf16[1,2,32,8,3584]{4,3,2,0,1:T(8,128)(2,1)S(1)} all-to-all(bf16[1,2,32,8,3584]{4,3,2,0,1:T(8,128)(2,1)S(1)} %copy.27), channel_id=1, replica_groups=mesh['expert'=32,'tensor'=4,'dp'=2] {'dp'}, dimensions={1} | all-to-all | bytes 7340032 | tf_op jit(solution)/shard_map/all_to_all | solution.py:59
  20.1 0.5 copy.28
  20.6 93.1 %all_to_all.21 = bf16[1,2,32,8,3584]{4,3,1,0,2:T(8,128)(2,1)S(1)} all-to-all(bf16[1,2,32,8,3584]{4,3,1,0,2:T(8,128)(2,1)S(1)} %copy.28), channel_id=1, replica_groups=mesh['expert'=32,'tensor'=4,'dp'=2] {'expert'}, dimensions={2} | all-to-all | bytes 7340032 | tf_op jit(solution)/shard_map/all_to_all | solution.py:12
  113.7 0.0 copy-start.1
  113.7 0.3 copy.29
  114.0 1.8 copy-done.1
  115.8 0.0 copy-start.2
  115.8 2.9 %fusion.13 = bf16[1,512,512]{2,1,0:T(8,128)(2,1)} fusion(bf16[512,3584]{1,0:T(8,128)(2,1)S(1)} %bitcast.71, bf16[1,3584,512]{2,1,0:T(8,128)(2,1)S(1)} %copy-done.1), kind=kOutput, calls=%fused_computation.15 | convolution fusion | flops 1879310336 | bytes 7864320 | tf_op jit(solution)/shard_map/lrh,lhf->lrf/dot_general | solution.py:64
  118.6 0.0 copy-done.2
  118.6 2.9 %fusion.16 = bf16[1,512,512]{2,1,0:T(8,128)(2,1)} fusion(bf16[512,3584]{1,0:T(8,128)(2,1)S(1)} %bitcast.72, bf16[1,3584,512]{2,1,0:T(8,128)(2,1)S(1)} %copy-done.2), kind=kOutput, calls=%fused_computation.16 | convolution fusion | flops 1879310336 | bytes 7864320 | tf_op jit(solution)/shard_map/lrh,lhf->lrf/dot_general | solution.py:63
  121.5 0.0 all-reduce.3.cloned.1.call-update
  121.6 0.0 reduce-scatter.4.cloned.1.call-start
  121.6 29.0 %all-reduce.3.cloned.1.call-done = (bf16[1,512,512]{2,1,0:T(8,128)(2,1)}, bf16[1,512,512]{2,1,0:T(8,128)(2,1)}) async-done(((bf16[1,512,512]{2,1,0:T(8,128)(2,1)}, bf16[1,512,512]{2,1,0:T(8,128)(2,1)}), (bf16[1,512,512]{2,1,0:T(8,128)(2,1)}, bf16[1,512,512]{2,1,0:T(8,128)(2,1)})) %all-reduce.3.cloned.1.call-update) | async-done | bytes 1048592 | tf_op jit(solution)/shard_map/psum | solution.py:67
  150.6 6.4 %fusion.1 = bf16[1,512,3584]{2,1,0:T(8,128)(2,1)} fusion(bf16[1,512,3584]{2,1,0:T(8,128)(2,1)} %param.11, bf16[1,512,512]{2,1,0:T(8,128)(2,1)} %get-tuple-element.5, bf16[1,512,512]{2,1,0:T(8,128)(2,1)} %get-tuple-element.6), kind=kOutput, calls=%fused_computation.3 | convolution fusion | flops 1882980352 | bytes 8388608 | tf_op jit(solution)/shard_map/lrf,lfh->lrh/dot_general | solution.py:70
  157.0 16.5 %copy.38 = bf16[1,512,3584]{1,0,2:T(2,128)(2,1)} copy(bf16[1,512,3584]{2,1,0:T(8,128)(2,1)} %fusion.1) | data formatting | bytes 7340032
  173.5 6.1 %copy.51 = bf16[3584,1,512]{2,0,1:T(8,128)(2,1)} copy(bf16[3584,1,512]{2,1,0:T(2,128)(2,1)} %bitcast.69) | data formatting | bytes 7340032
  179.6 0.0 reduce-scatter.4.cloned.1.call-update
  179.6 45.8 %reduce-scatter.4.cloned.1.call-done = bf16[896,512]{1,0:T(8,128)(2,1)} async-done(((bf16[3584,512]{1,0:T(8,128)(2,1)}), bf16[896,512]{1,0:T(8,128)(2,1)}) %reduce-scatter.4.cloned.1.call-update) | async-done | bytes 917520
  225.5 2.1 reshape_bitcast_fusion
  227.6 0.0 copy-start
  227.6 1.3 copy.39
  228.9 1.0 copy.30
  229.9 9.6 %all-to-all-start.2 = ((bf16[1,2,32,8,896]{4,3,1,0,2:T(8,128)(2,1)}), bf16[1,2,32,8,896]{4,3,1,0,2:T(8,128)(2,1)S(1)}, u32[]{:S(2)}, u32[]{:S(2)}) async-start(bf16[1,2,32,8,896]{4,3,1,0,2:T(8,128)(2,1)} %copy.30), calls=%async_computation.2 | async-start | bytes 1835008 | tf_op jit(solution)/shard_map/all_to_all | solution.py:12
  239.5 0.0 copy-done
  239.5 0.1 copy.24
  239.6 0.2 convolution_convert_fusion.3
  239.8 23.1 %all-to-all-done.2 = bf16[1,2,32,8,896]{4,3,1,0,2:T(8,128)(2,1)S(1)} async-done(((bf16[1,2,32,8,896]{4,3,1,0,2:T(8,128)(2,1)}), bf16[1,2,32,8,896]{4,3,1,0,2:T(8,128)(2,1)S(1)}, u32[]{:S(2)}, u32[]{:S(2)}) %all-to-all-start.2) | async-done | bytes 917536 | tf_op jit(solution)/shard_map/all_to_all | solution.py:12
  263.0 0.2 copy.31
  263.1 7.2 %all_to_all.22 = bf16[1,2,32,8,896]{4,2,3,0,1:T(8,128)(2,1)S(1)} all-to-all(bf16[1,2,32,8,896]{4,2,3,0,1:T(8,128)(2,1)S(1)} %copy.31), channel_id=1, replica_groups=mesh['expert'=32,'tensor'=4,'dp'=2] {'dp'}, dimensions={1} | all-to-all | bytes 1835008 | tf_op jit(solution)/shard_map/all_to_all | solution.py:80
  270.3 0.4 fusion.19
  270.8 0.7 copy.33
  (2 shorter events, 0.0 us)
Async XLA Ops:
  6.5 144.1 %all-reduce.3.cloned.1.call-start = ((), (), s32[]{:S(2)}) async-start(), calls=%async_computation.6 | async-start | bytes 2097152 | tf_op jit(solution)/shard_map/psum | solution.py:67
  113.7 2.0 copy-start.1
  115.8 2.9 %copy-start.2 = (bf16[1,3584,512]{2,1,0:T(8,128)(2,1)S(1)}, bf16[1,3584,512]{2,1,0:T(8,128)(2,1)}, u32[]{:S(2)}) copy-start(bf16[1,3584,512]{2,1,0:T(8,128)(2,1)} %param.9) | copy-start | bytes 11010052
  121.6 103.9 %reduce-scatter.4.cloned.1.call-start = ((), (), s32[]{:S(2)}) async-start(), calls=%async_computation.5 | async-start | bytes 4587520
  227.6 11.9 %copy-start = (f32[16,8]{0,1:T(8,128)S(1)}, f32[16,8]{0,1:T(8,128)}, u32[]{:S(2)}) copy-start(f32[16,8]{0,1:T(8,128)} %param.8) | copy-start | bytes 1540
  229.9 33.1 %all-to-all-start.2 = ((bf16[1,2,32,8,896]{4,3,1,0,2:T(8,128)(2,1)}), bf16[1,2,32,8,896]{4,3,1,0,2:T(8,128)(2,1)S(1)}, u32[]{:S(2)}, u32[]{:S(2)}) async-start(bf16[1,2,32,8,896]{4,3,1,0,2:T(8,128)(2,1)} %copy.30), calls=%async_computation.2 | async-start | bytes 1835008 | tf_op jit(solution)/shard_map/all_to_all | solution.py:12
Sparse Core Ops, SparseCore 0:
  121.7 28.8 all-reduce.2
  179.7 45.6 reduce-scatter.3
where the time goes:
time: 279 us; the launch traced here: 278 us
  blocking collectives  110 us (39%)
  waiting for transfers between devices  98 us (35%)
  local copies, waits for them, and re-layouts  31.8 us (11%)
  matrix products  15.1 us (5%)
  between operations  13.5 us (5%)
  starting transfers between devices  9.6 us (3%)
    all_to_all x1, blocking collectives, route_over_experts(): lax.all_to_all(blocks, 'expert', split_axis=2, concat_axis=2, tiled=True)  93.1 us
    unnamed x3, waiting for transfers between devices  45.9 us
    psum x1, waiting for transfers between devices, on_device(): lax.psum(up.astype(jnp.bfloat16), 'dp').astype(jnp.float32)  29 us
    unnamed x11, local copies, waits for them, and re-layouts  28.5 us
    all_to_all x1, waiting for transfers between devices, route_over_experts(): lax.all_to_all(blocks, 'expert', split_axis=2, concat_axis=2, tiled=True)  23.1 us
    all_to_all x1, starting transfers between devices, route_over_experts(): lax.all_to_all(blocks, 'expert', split_axis=2, concat_axis=2, tiled=True)  9.56 us
    all_to_all x1, blocking collectives, on_device(): lax.all_to_all(outgoing, 'dp', split_axis=1, concat_axis=1, tiled=True)  9.55 us
    all_to_all x1, blocking collectives, on_device(): lax.all_to_all(returned, 'dp', split_axis=1, concat_axis=1, tiled=True)  7.17 us
  transfers between devices with their start and end apart: 3, of which 3 were waited for; matrix products, arithmetic and copies ran while one was open for 0% of the time, Pallas kernels for 0%

commit v1 on v0

--- a/solution.py
+++ b/solution.py
@@ -64,7 +64,7 @@
     up = jnp.einsum("lrh,lhf->lrf", arrived, up_weight, preferred_element_type=jnp.float32)
     gate, up = (
         lax.psum(gate.astype(jnp.bfloat16), "dp").astype(jnp.float32),
-        lax.psum(up.astype(jnp.bfloat16), "dp").astype(jnp.float32),
+        jnp.sum(lax.all_gather(up.astype(jnp.bfloat16), "dp"), axis=0).astype(jnp.float32),
     )
     hidden = (jax.nn.silu(gate) * up).astype(jnp.bfloat16)
     partial_value = jnp.einsum(

time: 279 us -> 295 us (1.057)
  waiting for transfers between devices: 98 us -> 108 us
  matrix products: 15.1 us -> 18.1 us
    all_gather x0 -> x1, waiting for transfers between devices: none -> 6.84 us  [on_device(): lax.all_gather(up.astype(jnp.bfloat16), 'dp')]
    dot_general x1, matrix products: 2.89 us -> 6.02 us  [on_device(): jnp.einsum('lrh,lhf->lrf', arrived, gate_weight, preferred_element_type=j...]
    unnamed x3 -> x4, waiting for transfers between devices: 45.9 us -> 45.9 us
  transfers between devices with their start and end apart: 3 -> 4, of which waited for: 3 -> 4; matrix products, arithmetic and copies ran while one was open for 0% -> 3% of each run, Pallas kernels for 0% -> 0%
where the time goes in v1:
time: 295 us; the launch traced here: 294 us
  blocking collectives  110 us (37%)
  waiting for transfers between devices  108 us (37%)
  local copies, waits for them, and re-layouts  33.1 us (11%)
  matrix products  18.1 us (6%)
  between operations  13.2 us (4%)
  starting transfers between devices  9.65 us (3%)
    all_to_all x1, blocking collectives, route_over_experts(): lax.all_to_all(blocks, 'expert', split_axis=2, concat_axis=2, tiled=True)  93.1 us
    unnamed x4, waiting for transfers between devices  45.9 us
    psum x1, waiting for transfers between devices, on_device(): lax.psum(gate.astype(jnp.bfloat16), 'dp').astype(jnp.float32)  31.8 us
    unnamed x11, local copies, waits for them, and re-layouts  29.8 us
    all_to_all x1, waiting for transfers between devices, route_over_experts(): lax.all_to_all(blocks, 'expert', split_axis=2, concat_axis=2, tiled=True)  23.1 us
    all_to_all x1, starting transfers between devices, route_over_experts(): lax.all_to_all(blocks, 'expert', split_axis=2, concat_axis=2, tiled=True)  9.56 us
    all_to_all x1, blocking collectives, on_device(): lax.all_to_all(outgoing, 'dp', split_axis=1, concat_axis=1, tiled=True)  9.55 us
    all_to_all x1, blocking collectives, on_device(): lax.all_to_all(returned, 'dp', split_axis=1, concat_axis=1, tiled=True)  7.17 us
  transfers between devices with their start and end apart: 4, of which 4 were waited for; matrix products, arithmetic and copies ran while one was open for 3% of the time, Pallas kernels for 0%

profile of v1, /device:TPU:1, one launch (start us, length us, event | category | flops | bytes accessed | tf_op | source)
XLA Modules:
  0.0 293.6 jit_solution(17217202902236917258)
XLA Ops:
  6.5 0.0 all-gather.3.cloned.1.call-start
  6.5 0.8 copy.22
  7.3 0.1 eq.28
  7.4 0.1 fusion.28
  7.5 0.2 reduce_window_sum.12
  7.7 0.2 select_reduce_fusion
  7.8 0.1 eq.32
  7.9 0.2 fusion.17
  8.1 0.1 copy.34
  8.3 2.0 fusion
  10.3 0.3 copy.27
  10.6 9.5 %all_to_all.20 = bf16[1,2,32,8,3584]{4,3,2,0,1:T(8,128)(2,1)S(1)} all-to-all(bf16[1,2,32,8,3584]{4,3,2,0,1:T(8,128)(2,1)S(1)} %copy.27), channel_id=1, replica_groups=mesh['expert'=32,'tensor'=4,'dp'=2] {'dp'}, dimensions={1} | all-to-all | bytes 7340032 | tf_op jit(solution)/shard_map/all_to_all | solution.py:59
  20.1 0.5 copy.28
  20.6 93.1 %all_to_all.21 = bf16[1,2,32,8,3584]{4,3,1,0,2:T(8,128)(2,1)S(1)} all-to-all(bf16[1,2,32,8,3584]{4,3,1,0,2:T(8,128)(2,1)S(1)} %copy.28), channel_id=1, replica_groups=mesh['expert'=32,'tensor'=4,'dp'=2] {'expert'}, dimensions={2} | all-to-all | bytes 7340032 | tf_op jit(solution)/shard_map/all_to_all | solution.py:12
  113.7 0.0 copy-start.2
  113.7 0.3 copy.29
  114.0 0.0 copy-start
  114.0 1.9 copy-done
  115.9 1.2 copy-done.2
  117.1 2.9 fusion.10
  119.9 0.0 all-gather.3.cloned.1.call-update
  120.0 0.0 all-reduce.2.cloned.1.call-start
  120.0 6.0 %fusion.13 = bf16[1,512,512]{2,1,0:T(8,128)(2,1)} fusion(bf16[512,3584]{1,0:T(8,128)(2,1)} %bitcast.75, bf16[1,3584,512]{2,1,0:T(8,128)(2,1)} %param.9), kind=kOutput, calls=%fused_computation.15 | convolution fusion | flops 1879310336 | bytes 7864320 | tf_op jit(solution)/shard_map/lrh,lhf->lrf/dot_general | solution.py:63
  126.0 0.0 all-reduce.2.cloned.1.call-update
  126.1 0.0 reduce-scatter.4.cloned.1.call-start
  126.1 6.8 %all-gather.3.cloned.1.call-done = bf16[1024,512]{1,0:T(8,128)(2,1)} async-done(((bf16[512,512]{1,0:T(8,128)(2,1)}), bf16[1024,512]{1,0:T(8,128)(2,1)}) %all-gather.3.cloned.1.call-update) | async-done | bytes 1048592 | tf_op jit(solution)/shard_map/all_gather | solution.py:67
  133.0 1.7 reduce.2
  134.6 31.8 %all-reduce.2.cloned.1.call-done = bf16[1,512,512]{2,1,0:T(8,128)(2,1)} async-done(((bf16[1,512,512]{2,1,0:T(8,128)(2,1)}), bf16[1,512,512]{2,1,0:T(8,128)(2,1)}) %all-reduce.2.cloned.1.call-update) | async-done | bytes 524304 | tf_op jit(solution)/shard_map/psum | solution.py:66
  166.4 6.2 %fusion.1 = bf16[1,512,3584]{2,1,0:T(8,128)(2,1)} fusion(bf16[1,512,3584]{2,1,0:T(8,128)(2,1)} %param.11, bf16[1,512,512]{2,1,0:T(8,128)(2,1)} %all-reduce.2.cloned.1.call-done, bf16[512,512]{1,0:T(8,128)(2,1)S(1)} %reduce.2), kind=kOutput, calls=%fused_computation.3 | convolution fusion | flops 1882980352 | bytes 8388608 | tf_op jit(solution)/shard_map/lrf,lfh->lrh/dot_general | solution.py:70
  172.6 16.5 %copy.38 = bf16[1,512,3584]{1,0,2:T(2,128)(2,1)} copy(bf16[1,512,3584]{2,1,0:T(8,128)(2,1)} %fusion.1) | data formatting | bytes 7340032
  189.1 6.1 %copy.51 = bf16[3584,1,512]{2,0,1:T(8,128)(2,1)} copy(bf16[3584,1,512]{2,1,0:T(2,128)(2,1)} %bitcast.72) | data formatting | bytes 7340032
  195.2 0.0 reduce-scatter.4.cloned.1.call-update
  195.2 45.8 %reduce-scatter.4.cloned.1.call-done = bf16[896,512]{1,0:T(8,128)(2,1)} async-done(((bf16[3584,512]{1,0:T(8,128)(2,1)}), bf16[896,512]{1,0:T(8,128)(2,1)}) %reduce-scatter.4.cloned.1.call-update) | async-done | bytes 917520
  241.1 2.1 reshape_bitcast_fusion
  243.2 0.0 copy-start.1
  243.2 1.3 copy.39
  244.5 1.0 copy.30
  245.5 9.6 %all-to-all-start.2 = ((bf16[1,2,32,8,896]{4,3,1,0,2:T(8,128)(2,1)}), bf16[1,2,32,8,896]{4,3,1,0,2:T(8,128)(2,1)S(1)}, u32[]{:S(2)}, u32[]{:S(2)}) async-start(bf16[1,2,32,8,896]{4,3,1,0,2:T(8,128)(2,1)} %copy.30), calls=%async_computation.2 | async-start | bytes 1835008 | tf_op jit(solution)/shard_map/all_to_all | solution.py:12
  255.1 0.0 copy-done.1
  255.1 0.1 copy.24
  255.2 0.2 convolution_convert_fusion.3
  255.4 23.1 %all-to-all-done.2 = bf16[1,2,32,8,896]{4,3,1,0,2:T(8,128)(2,1)S(1)} async-done(((bf16[1,2,32,8,896]{4,3,1,0,2:T(8,128)(2,1)}), bf16[1,2,32,8,896]{4,3,1,0,2:T(8,128)(2,1)S(1)}, u32[]{:S(2)}, u32[]{:S(2)}) %all-to-all-start.2) | async-done | bytes 917536 | tf_op jit(solution)/shard_map/all_to_all | solution.py:12
  278.6 0.2 copy.31
  278.8 7.2 %all_to_all.22 = bf16[1,2,32,8,896]{4,2,3,0,1:T(8,128)(2,1)S(1)} all-to-all(bf16[1,2,32,8,896]{4,2,3,0,1:T(8,128)(2,1)S(1)} %copy.31), channel_id=1, replica_groups=mesh['expert'=32,'tensor'=4,'dp'=2] {'dp'}, dimensions={1} | all-to-all | bytes 1835008 | tf_op jit(solution)/shard_map/all_to_all | solution.py:80
  285.9 0.4 fusion.16
  286.4 0.7 copy.33
  (2 shorter events, 0.0 us)
Async XLA Ops:
  6.5 126.4 %all-gather.3.cloned.1.call-start = ((), (), s32[]{:S(2)}) async-start(), calls=%async_computation.6 | async-start | bytes 1572864 | tf_op jit(solution)/shard_map/all_gather | solution.py:67
  113.7 3.4 %copy-start.2 = (bf16[1,3584,512]{2,1,0:T(8,128)(2,1)S(1)}, bf16[1,3584,512]{2,1,0:T(8,128)(2,1)}, u32[]{:S(2)}) copy-start(bf16[1,3584,512]{2,1,0:T(8,128)(2,1)} %param.10) | copy-start | bytes 11010052
  114.0 1.9 copy-start
  120.0 46.4 %all-reduce.2.cloned.1.call-start = ((), (), s32[]{:S(2)}) async-start(), calls=%async_computation.5 | async-start | bytes 1048576 | tf_op jit(solution)/shard_map/psum | solution.py:66
  126.1 115.0 %reduce-scatter.4.cloned.1.call-start = ((), (), s32[]{:S(2)}) async-start(), calls=%async_computation.7 | async-start | bytes 4587520
  243.2 11.9 %copy-start.1 = (f32[16,8]{0,1:T(8,128)S(1)}, f32[16,8]{0,1:T(8,128)}, u32[]{:S(2)}) copy-start(f32[16,8]{0,1:T(8,128)} %param.8) | copy-start | bytes 1540
  245.5 33.1 %all-to-all-start.2 = ((bf16[1,2,32,8,896]{4,3,1,0,2:T(8,128)(2,1)}), bf16[1,2,32,8,896]{4,3,1,0,2:T(8,128)(2,1)S(1)}, u32[]{:S(2)}, u32[]{:S(2)}) async-start(bf16[1,2,32,8,896]{4,3,1,0,2:T(8,128)(2,1)} %copy.30), calls=%async_computation.2 | async-start | bytes 1835008 | tf_op jit(solution)/shard_map/all_to_all | solution.py:12
Sparse Core Ops, SparseCore 0:
  120.1 12.8 all-gather.2
  135.5 30.7 all-reduce.1
  195.4 45.6 reduce-scatter.3
